TPU v7x, 128 devices: a whole 4x4x4 slice. The times are simulated.
128 devices in a mesh: stream: 8 (over x, z_lo), span: 16 (over y, z_hi, core).
Axes of the slice: x: 4, y: 4, z: 4 (z_hi: 2, z_lo: 2; z = z_hi * 2 + z_lo), core: 2. Of those that a mesh axis runs over, the one named last changes fastest.
Arguments:
- right_side: float32 [4, 262144], P(None, ('stream', 'span')), may hold values from -5 to 6
- fine_values: float32 [8, 4, 4, 262144], P(None, None, None, ('stream', 'span')), as said below
- fine_columns: int32 [8, 262144], P(None, ('stream', 'span')), may hold values from 0 to 2303, as said below
- fine_sends: int32 [4, 8192], P(None, ('stream', 'span')), may hold values from 0 to 2047, as said below
- fine_order: int32 [128, 2048], P(('stream', 'span')), may hold values from 0 to 2047, each once within a row
- fine_weights: float32 [4, 4, 262144], P(None, None, ('stream', 'span')), may hold values from -0.6 to 1.2
- middle_values: float32 [8, 4, 4, 65536], P(None, None, None, ('stream', 'span')), as said below
- middle_columns: int32 [8, 65536], P(None, ('stream', 'span')), may hold values from 0 to 767, as said below
- middle_sends: int32 [4, 8192], P(None, ('stream', 'span')), may hold values from 0 to 511, as said below
- middle_order: int32 [128, 512], P(('stream', 'span')), may hold values from 0 to 511, each once within a row
- middle_weights: float32 [4, 4, 65536], P(None, None, ('stream', 'span')), may hold values from -0.6 to 1.2
- coarsest_values: float32 [8, 4, 4, 16384], P(None, None, None, ('stream', 'span')), as said below
- coarsest_columns: int32 [8, 16384], P(None, ('stream', 'span')), may hold values from 0 to 2047, as said below
Outputs:
- solution: float32 [4, 262144], P(None, ('stream', 'span'))
- residual: float32 [4, 262144], P(None, ('stream', 'span'))
Inputs may be any that keep to these rules, and one draw needn't show every extreme that they name: `fine_sends`: entry [d, p * 64 + s] is a local row block of device p sent in direction d (0: lower stream index, 1: higher stream index, 2: lower span index, 3: higher span index). Each list has a length of at most 64, which differs between devices and directions and is 64 on some device; rows may repeat within a list, and the slots at or after the length repeat the list's slot 0 as padding. `middle_sends`: as for the first level, with local row blocks of the second level. `fine_columns`: block k = 0 of row block n names its own local row. Entries below 2048 are local row blocks; an entry 2048 + e * 64 + s names slot s of halo block e. Where halo block e has a sending device, s is below the length of that device's list; where it has none (the block is zero), s may be any slot below 64. `middle_columns`: as for the first level with 512 local row blocks. `coarsest_columns`: block k = 0 names the row block itself within its slab; the others name row blocks of the same slab. `fine_values`: each diagonal entry of the k = 0 block is 1 or more, and the other 31 entries of its row over all 8 blocks have absolute values summing to at most 0.9 times it. `middle_values`: as for the first level. `coarsest_values`: as for the first level.
All inputs are finite; a program needn't handle non-finite values.
Results may differ from a plain program's by a relative error of at most 0.0003.
Values sent between devices are 32-bit elements; how exact they have to be, the bound alone decides.
A program may use at most 64 MiB of HBM per device.

v0:
```python
import math
import jax
import jax.numpy as jnp
from jax import lax
from jax.sharding import PartitionSpec as P

KSM = 3
KC = 4
CHEB_CENTRE = 1.0
CHEB_RADIUS = 0.9


def padded(cells, sides, width, closed):
    for axis, dim in sides:
        count = lax.axis_size(axis)
        ends = count if closed else count - 1
        head = lax.slice_in_dim(cells, 0, width, axis=dim)
        tail = lax.slice_in_dim(cells, cells.shape[dim] - width, cells.shape[dim], axis=dim)
        cells = jnp.concatenate(
            [
                lax.ppermute(tail, axis, [(i, (i + 1) % count) for i in range(ends)]),
                cells,
                lax.ppermute(head, axis, [((i + 1) % count, i) for i in range(ends)]),
            ],
            axis=dim,
        )
    return cells


def chebyshev(operate, inverse_diag, target, initial, degree):
    sigma_value = CHEB_CENTRE / CHEB_RADIUS
    rho_prev = 1.0 / sigma_value
    if initial is None:
        iterate = jnp.zeros_like(target)
        current = target
    else:
        iterate = initial
        current = target - operate(initial)
    update = inverse_diag * current / CHEB_CENTRE
    iterate = iterate + update
    for _ in range(degree - 1):
        rho_next = 1.0 / (2.0 * sigma_value - rho_prev)
        current = target - operate(iterate)
        update = rho_next * rho_prev * update + 2.0 * rho_next / CHEB_RADIUS * (
            inverse_diag * current
        )
        iterate = iterate + update
        rho_prev = rho_next
    return iterate


def inverse_diagonal(values):
    identity = jnp.eye(4, dtype=values.dtype)
    return 1.0 / jnp.sum(values[0] * identity[:, :, None], axis=1)


def split_parts(vector):
    high_part = vector.astype(jnp.bfloat16)
    rest_part = vector - lax.optimization_barrier(high_part).astype(jnp.float32)
    middle_part = rest_part.astype(jnp.bfloat16)
    low_part = (rest_part - lax.optimization_barrier(middle_part).astype(jnp.float32)).astype(
        jnp.bfloat16
    )
    return jnp.concatenate([high_part, middle_part, low_part], axis=0)


def join_parts(product, row_count):
    return product[:row_count] + product[row_count : 2 * row_count] + product[2 * row_count :]


def pick_columns(vector, index_flat):
    parts = split_parts(vector)
    width = parts.shape[1]
    total = index_flat.shape[0]
    block_size = math.gcd(total, 2048)
    places = jnp.arange(width, dtype=jnp.int32)[:, None]

    def one_block(index_block):
        select = (places == index_block[None, :]).astype(jnp.bfloat16)
        return jnp.dot(parts, select, preferred_element_type=jnp.float32)

    picked = lax.map(one_block, index_flat.reshape(total // block_size, block_size))
    picked = jnp.moveaxis(picked, 0, 1).reshape(parts.shape[0], total)
    return join_parts(picked, vector.shape[0])


def extend(vector, send_rows):
    halo_width = send_rows.shape[1]
    outgoing = pick_columns(vector, send_rows.reshape(-1)).reshape(4, 4, halo_width)
    stream_pair = jnp.concatenate([outgoing[:, 0], outgoing[:, 1]], axis=1)
    span_pair = jnp.concatenate([outgoing[:, 2], outgoing[:, 3]], axis=1)
    stream_ext = padded(stream_pair, (("stream", 1),), halo_width, True)
    span_ext = padded(span_pair, (("span", 1),), halo_width, False)
    return jnp.concatenate(
        [
            vector,
            stream_ext[:, :halo_width],
            stream_ext[:, 3 * halo_width :],
            span_ext[:, :halo_width],
            span_ext[:, 3 * halo_width :],
        ],
        axis=1,
    )


def block_product(values, gathered):
    return jnp.einsum("kijn,jkn->in", values, gathered, precision=lax.Precision.HIGHEST)


def apply_level(vector, values, columns, send_rows):
    extended_vec = extend(vector, send_rows)
    picked = pick_columns(extended_vec, columns.reshape(-1)).reshape(
        4, columns.shape[0], columns.shape[1]
    )
    return block_product(values, picked)


def membership(order_rows):
    row_count = order_rows.shape[0]
    grouped = order_rows.reshape(row_count // 4, 4)
    places = jnp.arange(row_count, dtype=jnp.int32)[:, None, None]
    return jnp.any(places == grouped[None, :, :], axis=2).astype(jnp.bfloat16)


def restrict(fine_vec, weights, member):
    product = jnp.einsum("ijn,in->jn", weights, fine_vec, precision=lax.Precision.HIGHEST)
    parts = split_parts(product)
    return join_parts(jnp.dot(parts, member, preferred_element_type=jnp.float32), 4)


def prolong(coarse, weights, member):
    parts = split_parts(coarse)
    spread = join_parts(
        lax.dot_general(
            parts, member, (((1,), (1,)), ((), ())), preferred_element_type=jnp.float32
        ),
        4,
    )
    return jnp.einsum("ijn,jn->in", weights, spread, precision=lax.Precision.HIGHEST)


def per_device(
    right_side,
    fine_values,
    fine_columns,
    fine_sends,
    fine_order,
    fine_weights,
    middle_values,
    middle_columns,
    middle_sends,
    middle_order,
    middle_weights,
    coarsest_values,
    coarsest_columns,
):

    def fine_apply(vector):
        return apply_level(vector, fine_values, fine_columns, fine_sends)

    def middle_apply(vector):
        return apply_level(vector, middle_values, middle_columns, middle_sends)

    fine_inv = inverse_diagonal(fine_values)
    middle_inv = inverse_diagonal(middle_values)
    fine_member = membership(fine_order[0])
    middle_member = membership(middle_order[0])
    first_iter = chebyshev(fine_apply, fine_inv, right_side, None, KSM)
    fine_resid = right_side - fine_apply(first_iter)
    middle_rhs = restrict(fine_resid, fine_weights, fine_member)
    middle_iter = chebyshev(middle_apply, middle_inv, middle_rhs, None, KSM)
    middle_resid = middle_rhs - middle_apply(middle_iter)
    coarse_rhs = restrict(middle_resid, middle_weights, middle_member)
    own_rows = coarse_rhs.shape[1]
    group_rhs, group_values = (
        lax.all_gather(coarse_rhs, "span", axis=1, tiled=True),
        lax.all_gather(coarsest_values, "span", axis=3, tiled=True),
    )
    group_columns = lax.all_gather(coarsest_columns, "span", axis=1, tiled=True)

    def group_apply(vector):
        return block_product(group_values, vector[:, group_columns])

    group_iter = chebyshev(group_apply, inverse_diagonal(group_values), group_rhs, None, KC)
    coarse_iter = lax.dynamic_slice_in_dim(
        group_iter, lax.axis_index("span") * own_rows, own_rows, 1
    )
    middle_start = middle_iter + prolong(coarse_iter, middle_weights, middle_member)
    middle_final = chebyshev(middle_apply, middle_inv, middle_rhs, middle_start, KSM)
    fine_start = first_iter + prolong(middle_final, fine_weights, fine_member)
    solution = chebyshev(fine_apply, fine_inv, right_side, fine_start, KSM)
    residual = right_side - fine_apply(solution)
    return (solution, residual)


def solution(mesh):
    in_specs = (
        P(None, ("stream", "span")),
        P(None, None, None, ("stream", "span")),
        P(None, ("stream", "span")),
        P(None, ("stream", "span")),
        P(("stream", "span"), None),
        P(None, None, ("stream", "span")),
        P(None, None, None, ("stream", "span")),
        P(None, ("stream", "span")),
        P(None, ("stream", "span")),
        P(("stream", "span"), None),
        P(None, None, ("stream", "span")),
        P(None, None, None, ("stream", "span")),
        P(None, ("stream", "span")),
    )
    out_specs = (P(None, ("stream", "span")), P(None, ("stream", "span")))
    return jax.shard_map(
        per_device, mesh=mesh, in_specs=in_specs, out_specs=out_specs, check_vma=False
    )
```

profile of v0, /device:TPU:1, one launch (start us, length us, event | category | flops | bytes accessed | tf_op | source)
XLA Modules:
  0.0 694.1 jit_solution(7039340005807783666)
XLA Ops:
  10.9 48.5 %all-gather.2.cloned.1.call-done = f32[8,4,4,2048]{3,2,1,0:T(4,128)} async-done(((f32[8,4,4,128]{3,2,1,0:T(4,128)}), f32[8,4,4,2048]{3,2,1,0:T(4,128)}) %all-gather.2.cloned.1.call-update) | async-done | bytes 1048592 | tf_op jit(solution)/shard_map/all_gather | solution.py:177
  71.2 6.1 fusion.78
  77.6 30.0 %while.39 = (s32[]{:T(128)}, f32[8,12,2048]{2,1,0:T(8,128)S(1)}, s32[8,2048]{1,0:T(8,128)}, bf16[12,2304]{1,0:T(8,128)(2,1)S(1)}, s32[]{:T(128)}) while((s32[]{:T(128)}, f32[8,12,2048]{2,1,0:T(8,128)S(1)}, s32[8,2048]{1,0:T(8,128)}, bf16[12,2304]{1,0:T(8,128)(2,1)S(1)}, s32[]{:T(128)}) %tuple.301), condition=%wide.region_2.0_spmd.clone, body=%wide.region_1.0_spmd.clone.sunk | while | flops 117964800 | bytes 229445 | solution.py:82
  108.8 3.8 collective-permute-start.5
  112.6 5.7 collective-permute-start.6
  120.4 4.3 collective-permute-done.7
  125.0 23.3 %while.40 = (s32[]{:T(128)}, f32[8,12,2048]{2,1,0:T(8,128)S(1)}, s32[8,2048]{1,0:T(8,128)S(1)}, bf16[12,2304]{1,0:T(8,128)(2,1)S(1)}, s32[]{:T(128)}) while((s32[]{:T(128)}, f32[8,12,2048]{2,1,0:T(8,128)S(1)}, s32[8,2048]{1,0:T(8,128)S(1)}, bf16[12,2304]{1,0:T(8,128)(2,1)S(1)}, s32[]{:T(128)}) %tuple.347), condition=%wide.region_4.5_spmd.clone, body=%wide.region_3.0_spmd.clone.sunk | while | flops 117964800 | bytes 229445 | solution.py:82
  154.1 3.6 collective-permute-start.9
  157.7 26.1 %all_gather.11 = s32[8,2048]{1,0:T(8,128)} all-gather(s32[8,128]{1,0:T(8,128)S(1)} %copy-done.30), channel_id=1, replica_groups=mesh['stream'=8,'span'=16] {'span'}, dimensions={1}, use_global_device_ids=true | all-gather | bytes 69632 | tf_op jit(solution)/shard_map/all_gather | solution.py:179
  185.4 30.5 %while.41 = (s32[]{:T(128)}, f32[8,12,2048]{2,1,0:T(8,128)S(1)}, s32[8,2048]{1,0:T(8,128)S(1)}, bf16[12,2304]{1,0:T(8,128)(2,1)}, s32[]{:T(128)}) while((s32[]{:T(128)}, f32[8,12,2048]{2,1,0:T(8,128)S(1)}, s32[8,2048]{1,0:T(8,128)S(1)}, bf16[12,2304]{1,0:T(8,128)(2,1)}, s32[]{:T(128)}) %tuple.348), condition=%wide.region_7.8_spmd.clone, body=%wide.region_6.7_spmd.clone.sunk | while | flops 117964800 | bytes 211013 | solution.py:82
  185.4 3.9 fusion.397
  189.3 3.8 fusion.397
  193.1 3.8 fusion.397
  196.9 3.8 fusion.397
  200.7 3.8 fusion.397
  204.5 3.8 fusion.397
  208.3 3.8 fusion.397
  212.1 3.8 fusion.397
  218.4 3.6 collective-permute-start.13
  222.0 5.4 collective-permute-start.14
  236.9 3.6 collective-permute-start.17
  253.2 3.6 collective-permute-start.21
  261.4 4.3 collective-permute-done.23
  268.6 19.3 %all_gather.10 = f32[4,2048]{1,0:T(4,128)S(1)} all-gather(f32[4,128]{1,0:T(4,128)S(1)} %slice_add_fusion.58), channel_id=1, replica_groups=mesh['stream'=8,'span'=16] {'span'}, dimensions={1}, use_global_device_ids=true | all-gather | bytes 34816 | tf_op jit(solution)/shard_map/all_gather | solution.py:176
  289.0 54.8 %gather_fusion = f32[16384,4]{1,0:T(8,128)} fusion(f32[4,2048]{0,1:T(8,128)S(1)} %copy.181, s32[16384]{0:T(1024)S(1)} %broadcast_clamp_fusion), kind=kCustom, calls=%fused_computation | custom fusion | bytes 589824 | tf_op jit(solution)/shard_map/gather | solution.py:182
  343.8 5.3 copy.404
  351.8 60.0 %gather_fusion.1 = f32[16384,4]{1,0:T(8,128)} fusion(f32[4,2048]{0,1:T(8,128)S(1)} %copy.182, s32[16384]{0:T(1024)} %copy-done.5), kind=kCustom, calls=%fused_computation.1 | custom fusion | bytes 589824 | tf_op jit(solution)/shard_map/gather | solution.py:182
  411.8 5.2 copy.405
  419.2 60.0 %gather_fusion.2 = f32[16384,4]{1,0:T(8,128)} fusion(f32[4,2048]{0,1:T(8,128)S(1)} %copy.183, s32[16384]{0:T(1024)} %copy-done.5), kind=kCustom, calls=%fused_computation.2 | custom fusion | bytes 589824 | tf_op jit(solution)/shard_map/gather | solution.py:182
  479.3 5.3 copy.406
  486.3 3.6 collective-permute-start.25
  494.8 4.3 collective-permute-done.27
  502.2 3.6 collective-permute-start.29
  510.2 4.4 collective-permute-done.31
  517.7 3.6 collective-permute-start.33
  525.8 4.4 collective-permute-done.35
  534.5 3.6 collective-permute-start.37
  542.7 5.0 collective-permute-done.39
  548.0 23.3 %while.48 = (s32[]{:T(128)}, f32[8,12,2048]{2,1,0:T(8,128)S(1)}, s32[8,2048]{1,0:T(8,128)S(1)}, bf16[12,2304]{1,0:T(8,128)(2,1)S(1)}, s32[]{:T(128)}) while((s32[]{:T(128)}, f32[8,12,2048]{2,1,0:T(8,128)S(1)}, s32[8,2048]{1,0:T(8,128)S(1)}, bf16[12,2304]{1,0:T(8,128)(2,1)S(1)}, s32[]{:T(128)}) %tuple.349), condition=%wide.region_24.25_spmd.clone, body=%wide.region_23.24_spmd.clone.sunk | while | flops 117964800 | bytes 229445 | solution.py:82
  572.5 3.6 collective-permute-start.41
  580.5 5.3 collective-permute-done.43
  586.1 23.3 %while.49 = (s32[]{:T(128)}, f32[8,12,2048]{2,1,0:T(8,128)S(1)}, s32[8,2048]{1,0:T(8,128)S(1)}, bf16[12,2304]{1,0:T(8,128)(2,1)S(1)}, s32[]{:T(128)}) while((s32[]{:T(128)}, f32[8,12,2048]{2,1,0:T(8,128)S(1)}, s32[8,2048]{1,0:T(8,128)S(1)}, bf16[12,2304]{1,0:T(8,128)(2,1)S(1)}, s32[]{:T(128)}) %tuple.350), condition=%wide.region_26.27_spmd.clone, body=%wide.region_25.26_spmd.clone.sunk | while | flops 117964800 | bytes 229445 | solution.py:82
  610.6 3.6 collective-permute-start.45
  618.9 5.1 collective-permute-done.47
  624.3 23.3 %while.50 = (s32[]{:T(128)}, f32[8,12,2048]{2,1,0:T(8,128)S(1)}, s32[8,2048]{1,0:T(8,128)S(1)}, bf16[12,2304]{1,0:T(8,128)(2,1)S(1)}, s32[]{:T(128)}) while((s32[]{:T(128)}, f32[8,12,2048]{2,1,0:T(8,128)S(1)}, s32[8,2048]{1,0:T(8,128)S(1)}, bf16[12,2304]{1,0:T(8,128)(2,1)S(1)}, s32[]{:T(128)}) %tuple.351), condition=%wide.region_28.29_spmd.clone, body=%wide.region_27.28_spmd.clone.sunk | while | flops 117964800 | bytes 229445 | solution.py:82
  648.8 3.6 collective-permute-start.49
  656.8 5.3 collective-permute-done.51
  662.5 23.3 %while.51 = (s32[]{:T(128)}, f32[8,12,2048]{2,1,0:T(8,128)S(1)}, s32[8,2048]{1,0:T(8,128)S(1)}, bf16[12,2304]{1,0:T(8,128)(2,1)S(1)}, s32[]{:T(128)}) while((s32[]{:T(128)}, f32[8,12,2048]{2,1,0:T(8,128)S(1)}, s32[8,2048]{1,0:T(8,128)S(1)}, bf16[12,2304]{1,0:T(8,128)(2,1)S(1)}, s32[]{:T(128)}) %tuple.352), condition=%wide.region_30.31_spmd.clone, body=%wide.region_29.30_spmd.clone.sunk | while | flops 117964800 | bytes 229445 | solution.py:82
  (558 shorter events, 272.2 us)
Async XLA Ops:
  7.2 52.2 %all-gather.2.cloned.1.call-start = ((), (), s32[]{:S(2)}) async-start(), calls=%async_computation | async-start | bytes 1114112 | tf_op jit(solution)/shard_map/all_gather | solution.py:177
  62.6 14.6 %collective-permute-start = (f32[4,64]{1,0:T(4,128)S(1)}, f32[4,64]{1,0:T(4,128)S(1)}, u32[]{:S(2)}, u32[]{:S(2)}) collective-permute-start(f32[4,64]{1,0:T(4,128)S(1)} %bitcast.712), channel_id=1, source_target_pairs={{0,16},{16,32},{32,48},{48,64},{64,80},{80,96},{96,112},{112,0},{1... | collective-permute-start | bytes 3080 | tf_op jit(solution)/shard_map/ppermute | solution.py:21
  63.1 14.2 %collective-permute-start.1 = (f32[4,64]{1,0:T(4,128)S(1)}, f32[4,64]{1,0:T(4,128)S(1)}, u32[]{:S(2)}, u32[]{:S(2)}) collective-permute-start(f32[4,64]{1,0:T(4,128)S(1)} %bitcast.701), channel_id=1, source_target_pairs={{16,0},{32,16},{48,32},{64,48},{80,64},{96,80},{112,96},{0,112},{1... | collective-permute-start | bytes 3080 | tf_op jit(solution)/shard_map/ppermute | solution.py:23
  66.3 11.0 %collective-permute-start.2 = (f32[4,64]{1,0:T(4,128)S(1)}, f32[4,64]{1,0:T(4,128)S(1)}, u32[]{:S(2)}, u32[]{:S(2)}) collective-permute-start(f32[4,64]{1,0:T(4,128)S(1)} %bitcast.689), channel_id=1, source_target_pairs={{0,1},{1,2},{2,3},{3,4},{4,5},{5,6},{6,7},{7,8},{8,9},{9,10},{10,1... | collective-permute-start | bytes 3080 | tf_op jit(solution)/shard_map/ppermute | solution.py:21
  69.2 8.0 %collective-permute-start.3 = (f32[4,64]{1,0:T(4,128)S(1)}, f32[4,64]{1,0:T(4,128)S(1)}, u32[]{:S(2)}, u32[]{:S(2)}) collective-permute-start(f32[4,64]{1,0:T(4,128)S(1)} %bitcast.678), channel_id=1, source_target_pairs={{1,0},{2,1},{3,2},{4,3},{5,4},{6,5},{7,6},{8,7},{9,8},{10,9},{11,1... | collective-permute-start | bytes 3080 | tf_op jit(solution)/shard_map/ppermute | solution.py:23
  108.8 11.6 %collective-permute-start.4 = (f32[4,64]{1,0:T(4,128)S(1)}, f32[4,64]{1,0:T(4,128)S(1)}, u32[]{:S(2)}, u32[]{:S(2)}) collective-permute-start(f32[4,64]{1,0:T(4,128)S(1)} %bitcast.713), channel_id=1, source_target_pairs={{0,16},{16,32},{32,48},{48,64},{64,80},{80,96},{96,112},{112,0},{1... | collective-permute-start | bytes 3080 | tf_op jit(solution)/shard_map/ppermute | solution.py:21
  108.8 11.5 %collective-permute-start.5 = (f32[4,64]{1,0:T(4,128)S(1)}, f32[4,64]{1,0:T(4,128)S(1)}, u32[]{:S(2)}, u32[]{:S(2)}) collective-permute-start(f32[4,64]{1,0:T(4,128)S(1)} %bitcast.702), channel_id=1, source_target_pairs={{16,0},{32,16},{48,32},{64,48},{80,64},{96,80},{112,96},{0,112},{1... | collective-permute-start | bytes 3080 | tf_op jit(solution)/shard_map/ppermute | solution.py:23
  112.6 7.8 %collective-permute-start.6 = (f32[4,64]{1,0:T(4,128)S(1)}, f32[4,64]{1,0:T(4,128)S(1)}, u32[]{:S(2)}, u32[]{:S(2)}) collective-permute-start(f32[4,64]{1,0:T(4,128)S(1)} %bitcast.690), channel_id=1, source_target_pairs={{0,1},{1,2},{2,3},{3,4},{4,5},{5,6},{6,7},{7,8},{8,9},{9,10},{10,1... | collective-permute-start | bytes 3080 | tf_op jit(solution)/shard_map/ppermute | solution.py:21
  118.3 6.4 collective-permute-start.7
  149.5 34.9 %collective-permute-start.10 = (f32[4,64]{1,0:T(4,128)S(1)}, f32[4,64]{1,0:T(4,128)S(1)}, u32[]{:S(2)}, u32[]{:S(2)}) collective-permute-start(f32[4,64]{1,0:T(4,128)S(1)} %bitcast.714), channel_id=1, source_target_pairs={{0,1},{1,2},{2,3},{3,4},{4,5},{5,6},{6,7},{7,8},{8,9},{9,10},{10,1... | collective-permute-start | bytes 3080 | tf_op jit(solution)/shard_map/ppermute | solution.py:21
  152.1 32.3 %collective-permute-start.11 = (f32[4,64]{1,0:T(4,128)S(1)}, f32[4,64]{1,0:T(4,128)S(1)}, u32[]{:S(2)}, u32[]{:S(2)}) collective-permute-start(f32[4,64]{1,0:T(4,128)S(1)} %bitcast.703), channel_id=1, source_target_pairs={{1,0},{2,1},{3,2},{4,3},{5,4},{6,5},{7,6},{8,7},{9,8},{10,9},{11,1... | collective-permute-start | bytes 3080 | tf_op jit(solution)/shard_map/ppermute | solution.py:23
  154.0 30.4 %collective-permute-start.8 = (f32[4,64]{1,0:T(4,128)S(1)}, f32[4,64]{1,0:T(4,128)S(1)}, u32[]{:S(2)}, u32[]{:S(2)}) collective-permute-start(f32[4,64]{1,0:T(4,128)S(1)} %bitcast.691), channel_id=1, source_target_pairs={{0,16},{16,32},{32,48},{48,64},{64,80},{80,96},{96,112},{112,0},{1... | collective-permute-start | bytes 3080 | tf_op jit(solution)/shard_map/ppermute | solution.py:21
  154.1 30.3 %collective-permute-start.9 = (f32[4,64]{1,0:T(4,128)S(1)}, f32[4,64]{1,0:T(4,128)S(1)}, u32[]{:S(2)}, u32[]{:S(2)}) collective-permute-start(f32[4,64]{1,0:T(4,128)S(1)} %bitcast.680), channel_id=1, source_target_pairs={{16,0},{32,16},{48,32},{64,48},{80,64},{96,80},{112,96},{0,112},{1... | collective-permute-start | bytes 3080 | tf_op jit(solution)/shard_map/ppermute | solution.py:23
  218.3 13.0 %collective-permute-start.12 = (f32[4,64]{1,0:T(4,128)S(1)}, f32[4,64]{1,0:T(4,128)S(1)}, u32[]{:S(2)}, u32[]{:S(2)}) collective-permute-start(f32[4,64]{1,0:T(4,128)S(1)} %bitcast.704), channel_id=1, source_target_pairs={{0,16},{16,32},{32,48},{48,64},{64,80},{80,96},{96,112},{112,0},{1... | collective-permute-start | bytes 3080 | tf_op jit(solution)/shard_map/ppermute | solution.py:21
  218.4 12.9 %collective-permute-start.13 = (f32[4,64]{1,0:T(4,128)S(1)}, f32[4,64]{1,0:T(4,128)S(1)}, u32[]{:S(2)}, u32[]{:S(2)}) collective-permute-start(f32[4,64]{1,0:T(4,128)S(1)} %bitcast.692), channel_id=1, source_target_pairs={{16,0},{32,16},{48,32},{64,48},{80,64},{96,80},{112,96},{0,112},{1... | collective-permute-start | bytes 3080 | tf_op jit(solution)/shard_map/ppermute | solution.py:23
  222.0 9.3 %collective-permute-start.14 = (f32[4,64]{1,0:T(4,128)S(1)}, f32[4,64]{1,0:T(4,128)S(1)}, u32[]{:S(2)}, u32[]{:S(2)}) collective-permute-start(f32[4,64]{1,0:T(4,128)S(1)} %bitcast.681), channel_id=1, source_target_pairs={{0,1},{1,2},{2,3},{3,4},{4,5},{5,6},{6,7},{7,8},{8,9},{9,10},{10,1... | collective-permute-start | bytes 3080 | tf_op jit(solution)/shard_map/ppermute | solution.py:21
  227.3 6.4 collective-permute-start.15
  236.8 9.7 %collective-permute-start.16 = (f32[4,64]{1,0:T(4,128)S(1)}, f32[4,64]{1,0:T(4,128)S(1)}, u32[]{:S(2)}, u32[]{:S(2)}) collective-permute-start(f32[4,64]{1,0:T(4,128)S(1)} %bitcast.693), channel_id=1, source_target_pairs={{0,16},{16,32},{32,48},{48,64},{64,80},{80,96},{96,112},{112,0},{1... | collective-permute-start | bytes 3080 | tf_op jit(solution)/shard_map/ppermute | solution.py:21
  236.9 9.7 %collective-permute-start.17 = (f32[4,64]{1,0:T(4,128)S(1)}, f32[4,64]{1,0:T(4,128)S(1)}, u32[]{:S(2)}, u32[]{:S(2)}) collective-permute-start(f32[4,64]{1,0:T(4,128)S(1)} %bitcast.682), channel_id=1, source_target_pairs={{16,0},{32,16},{48,32},{64,48},{80,64},{96,80},{112,96},{0,112},{1... | collective-permute-start | bytes 3080 | tf_op jit(solution)/shard_map/ppermute | solution.py:23
  240.4 6.1 collective-permute-start.18
  243.7 6.4 collective-permute-start.19
  253.1 8.2 %collective-permute-start.20 = (f32[4,64]{1,0:T(4,128)S(1)}, f32[4,64]{1,0:T(4,128)S(1)}, u32[]{:S(2)}, u32[]{:S(2)}) collective-permute-start(f32[4,64]{1,0:T(4,128)S(1)} %bitcast.674), channel_id=1, source_target_pairs={{0,16},{16,32},{32,48},{48,64},{64,80},{80,96},{96,112},{112,0},{1... | collective-permute-start | bytes 3080 | tf_op jit(solution)/shard_map/ppermute | solution.py:21
  253.2 8.2 %collective-permute-start.21 = (f32[4,64]{1,0:T(4,128)S(1)}, f32[4,64]{1,0:T(4,128)S(1)}, u32[]{:S(2)}, u32[]{:S(2)}) collective-permute-start(f32[4,64]{1,0:T(4,128)S(1)} %bitcast.673), channel_id=1, source_target_pairs={{16,0},{32,16},{48,32},{64,48},{80,64},{96,80},{112,96},{0,112},{1... | collective-permute-start | bytes 3080 | tf_op jit(solution)/shard_map/ppermute | solution.py:23
  259.3 6.4 collective-permute-start.23
  486.2 8.6 %collective-permute-start.24 = (f32[4,64]{1,0:T(4,128)S(1)}, f32[4,64]{1,0:T(4,128)S(1)}, u32[]{:S(2)}, u32[]{:S(2)}) collective-permute-start(f32[4,64]{1,0:T(4,128)S(1)} %bitcast.716), channel_id=1, source_target_pairs={{0,16},{16,32},{32,48},{48,64},{64,80},{80,96},{96,112},{112,0},{1... | collective-permute-start | bytes 3080 | tf_op jit(solution)/shard_map/ppermute | solution.py:21
  486.3 8.5 %collective-permute-start.25 = (f32[4,64]{1,0:T(4,128)S(1)}, f32[4,64]{1,0:T(4,128)S(1)}, u32[]{:S(2)}, u32[]{:S(2)}) collective-permute-start(f32[4,64]{1,0:T(4,128)S(1)} %bitcast.706), channel_id=1, source_target_pairs={{16,0},{32,16},{48,32},{64,48},{80,64},{96,80},{112,96},{0,112},{1... | collective-permute-start | bytes 3080 | tf_op jit(solution)/shard_map/ppermute | solution.py:23
  489.9 4.9 collective-permute-start.26
  492.7 6.4 collective-permute-start.27
  502.1 8.1 %collective-permute-start.28 = (f32[4,64]{1,0:T(4,128)S(1)}, f32[4,64]{1,0:T(4,128)S(1)}, u32[]{:S(2)}, u32[]{:S(2)}) collective-permute-start(f32[4,64]{1,0:T(4,128)S(1)} %bitcast.717), channel_id=1, source_target_pairs={{0,16},{16,32},{32,48},{48,64},{64,80},{80,96},{96,112},{112,0},{1... | collective-permute-start | bytes 3080 | tf_op jit(solution)/shard_map/ppermute | solution.py:21
  502.2 8.0 %collective-permute-start.29 = (f32[4,64]{1,0:T(4,128)S(1)}, f32[4,64]{1,0:T(4,128)S(1)}, u32[]{:S(2)}, u32[]{:S(2)}) collective-permute-start(f32[4,64]{1,0:T(4,128)S(1)} %bitcast.707), channel_id=1, source_target_pairs={{16,0},{32,16},{48,32},{64,48},{80,64},{96,80},{112,96},{0,112},{1... | collective-permute-start | bytes 3080 | tf_op jit(solution)/shard_map/ppermute | solution.py:23
  508.3 6.4 collective-permute-start.31
  517.7 8.1 %collective-permute-start.32 = (f32[4,64]{1,0:T(4,128)S(1)}, f32[4,64]{1,0:T(4,128)S(1)}, u32[]{:S(2)}, u32[]{:S(2)}) collective-permute-start(f32[4,64]{1,0:T(4,128)S(1)} %bitcast.718), channel_id=1, source_target_pairs={{0,16},{16,32},{32,48},{48,64},{64,80},{80,96},{96,112},{112,0},{1... | collective-permute-start | bytes 3080 | tf_op jit(solution)/shard_map/ppermute | solution.py:21
  517.7 8.0 %collective-permute-start.33 = (f32[4,64]{1,0:T(4,128)S(1)}, f32[4,64]{1,0:T(4,128)S(1)}, u32[]{:S(2)}, u32[]{:S(2)}) collective-permute-start(f32[4,64]{1,0:T(4,128)S(1)} %bitcast.708), channel_id=1, source_target_pairs={{16,0},{32,16},{48,32},{64,48},{80,64},{96,80},{112,96},{0,112},{1... | collective-permute-start | bytes 3080 | tf_op jit(solution)/shard_map/ppermute | solution.py:23
  523.8 6.4 collective-permute-start.35
  534.4 8.3 %collective-permute-start.36 = (f32[4,64]{1,0:T(4,128)S(1)}, f32[4,64]{1,0:T(4,128)S(1)}, u32[]{:S(2)}, u32[]{:S(2)}) collective-permute-start(f32[4,64]{1,0:T(4,128)S(1)} %bitcast.719), channel_id=1, source_target_pairs={{0,16},{16,32},{32,48},{48,64},{64,80},{80,96},{96,112},{112,0},{1... | collective-permute-start | bytes 3080 | tf_op jit(solution)/shard_map/ppermute | solution.py:21
  534.5 8.2 %collective-permute-start.37 = (f32[4,64]{1,0:T(4,128)S(1)}, f32[4,64]{1,0:T(4,128)S(1)}, u32[]{:S(2)}, u32[]{:S(2)}) collective-permute-start(f32[4,64]{1,0:T(4,128)S(1)} %bitcast.709), channel_id=1, source_target_pairs={{16,0},{32,16},{48,32},{64,48},{80,64},{96,80},{112,96},{0,112},{1... | collective-permute-start | bytes 3080 | tf_op jit(solution)/shard_map/ppermute | solution.py:23
  538.1 4.7 collective-permute-start.38
  540.6 7.1 %collective-permute-start.39 = (f32[4,64]{1,0:T(4,128)S(1)}, f32[4,64]{1,0:T(4,128)S(1)}, u32[]{:S(2)}, u32[]{:S(2)}) collective-permute-start(f32[4,64]{1,0:T(4,128)S(1)} %bitcast.686), channel_id=1, source_target_pairs={{1,0},{2,1},{3,2},{4,3},{5,4},{6,5},{7,6},{8,7},{9,8},{10,9},{11,1... | collective-permute-start | bytes 3080 | tf_op jit(solution)/shard_map/ppermute | solution.py:23
  572.4 8.1 %collective-permute-start.40 = (f32[4,64]{1,0:T(4,128)S(1)}, f32[4,64]{1,0:T(4,128)S(1)}, u32[]{:S(2)}, u32[]{:S(2)}) collective-permute-start(f32[4,64]{1,0:T(4,128)S(1)} %bitcast.720), channel_id=1, source_target_pairs={{0,16},{16,32},{32,48},{48,64},{64,80},{80,96},{96,112},{112,0},{1... | collective-permute-start | bytes 3080 | tf_op jit(solution)/shard_map/ppermute | solution.py:21
  572.5 8.0 %collective-permute-start.41 = (f32[4,64]{1,0:T(4,128)S(1)}, f32[4,64]{1,0:T(4,128)S(1)}, u32[]{:S(2)}, u32[]{:S(2)}) collective-permute-start(f32[4,64]{1,0:T(4,128)S(1)} %bitcast.710), channel_id=1, source_target_pairs={{16,0},{32,16},{48,32},{64,48},{80,64},{96,80},{112,96},{0,112},{1... | collective-permute-start | bytes 3080 | tf_op jit(solution)/shard_map/ppermute | solution.py:23
  578.6 7.3 %collective-permute-start.43 = (f32[4,64]{1,0:T(4,128)S(1)}, f32[4,64]{1,0:T(4,128)S(1)}, u32[]{:S(2)}, u32[]{:S(2)}) collective-permute-start(f32[4,64]{1,0:T(4,128)S(1)} %bitcast.687), channel_id=1, source_target_pairs={{1,0},{2,1},{3,2},{4,3},{5,4},{6,5},{7,6},{8,7},{9,8},{10,9},{11,1... | collective-permute-start | bytes 3080 | tf_op jit(solution)/shard_map/ppermute | solution.py:23
  610.5 8.3 %collective-permute-start.44 = (f32[4,64]{1,0:T(4,128)S(1)}, f32[4,64]{1,0:T(4,128)S(1)}, u32[]{:S(2)}, u32[]{:S(2)}) collective-permute-start(f32[4,64]{1,0:T(4,128)S(1)} %bitcast.721), channel_id=1, source_target_pairs={{0,16},{16,32},{32,48},{48,64},{64,80},{80,96},{96,112},{112,0},{1... | collective-permute-start | bytes 3080 | tf_op jit(solution)/shard_map/ppermute | solution.py:21
  610.6 8.3 %collective-permute-start.45 = (f32[4,64]{1,0:T(4,128)S(1)}, f32[4,64]{1,0:T(4,128)S(1)}, u32[]{:S(2)}, u32[]{:S(2)}) collective-permute-start(f32[4,64]{1,0:T(4,128)S(1)} %bitcast.711), channel_id=1, source_target_pairs={{16,0},{32,16},{48,32},{64,48},{80,64},{96,80},{112,96},{0,112},{1... | collective-permute-start | bytes 3080 | tf_op jit(solution)/shard_map/ppermute | solution.py:23
  614.2 4.7 collective-permute-start.46
  616.7 7.3 %collective-permute-start.47 = (f32[4,64]{1,0:T(4,128)S(1)}, f32[4,64]{1,0:T(4,128)S(1)}, u32[]{:S(2)}, u32[]{:S(2)}) collective-permute-start(f32[4,64]{1,0:T(4,128)S(1)} %bitcast.688), channel_id=1, source_target_pairs={{1,0},{2,1},{3,2},{4,3},{5,4},{6,5},{7,6},{8,7},{9,8},{10,9},{11,1... | collective-permute-start | bytes 3080 | tf_op jit(solution)/shard_map/ppermute | solution.py:23
  648.7 8.1 %collective-permute-start.48 = (f32[4,64]{1,0:T(4,128)S(1)}, f32[4,64]{1,0:T(4,128)S(1)}, u32[]{:S(2)}, u32[]{:S(2)}) collective-permute-start(f32[4,64]{1,0:T(4,128)S(1)} %bitcast.722), channel_id=1, source_target_pairs={{0,16},{16,32},{32,48},{48,64},{64,80},{80,96},{96,112},{112,0},{1... | collective-permute-start | bytes 3080 | tf_op jit(solution)/shard_map/ppermute | solution.py:21
  648.8 8.0 %collective-permute-start.49 = (f32[4,64]{1,0:T(4,128)S(1)}, f32[4,64]{1,0:T(4,128)S(1)}, u32[]{:S(2)}, u32[]{:S(2)}) collective-permute-start(f32[4,64]{1,0:T(4,128)S(1)} %bitcast.715), channel_id=1, source_target_pairs={{16,0},{32,16},{48,32},{64,48},{80,64},{96,80},{112,96},{0,112},{1... | collective-permute-start | bytes 3080 | tf_op jit(solution)/shard_map/ppermute | solution.py:23
  654.9 7.3 %collective-permute-start.51 = (f32[4,64]{1,0:T(4,128)S(1)}, f32[4,64]{1,0:T(4,128)S(1)}, u32[]{:S(2)}, u32[]{:S(2)}) collective-permute-start(f32[4,64]{1,0:T(4,128)S(1)} %bitcast.694), channel_id=1, source_target_pairs={{1,0},{2,1},{3,2},{4,3},{5,4},{6,5},{7,6},{8,7},{9,8},{10,9},{11,1... | collective-permute-start | bytes 3080 | tf_op jit(solution)/shard_map/ppermute | solution.py:23
  (43 other events, 845.6 us)
Sparse Core Ops, SparseCore 0:
  10.3 49.1 all-gather.1
where the time goes:
time: 707 us; the launch traced here: 694 us
  local copies, waits for them, and re-layouts  209 us (30%)
  matrix products  188 us (27%)
  starting transfers between devices  114 us (16%)
  waiting for transfers between devices  97.8 us (14%)
  blocking collectives  45.4 us (6%)
  other arithmetic  22.8 us (3%)
  between operations  16.7 us (2%)
    dot_general x81, matrix products, one_block(): return jnp.dot(parts, select, preferred_element_type=jnp.float32)  187 us
    gather x3, local copies, waits for them, and re-layouts, group_apply(): return block_product(group_values, vector[:, group_columns])  175 us
    ppermute x26, starting transfers between devices, padded(): lax.ppermute(head, axis, [((i + 1) % count, i) for i in range(ends)])  72.1 us
    ppermute x26, waiting for transfers between devices, padded(): lax.ppermute(head, axis, [((i + 1) % count, i) for i in range(ends)])  48.6 us
    all_gather x1, waiting for transfers between devices, per_device(): lax.all_gather(coarsest_values, 'span', axis=3, tiled=True)  48.5 us
    ppermute x26, starting transfers between devices, padded(): lax.ppermute(tail, axis, [(i, (i + 1) % count) for i in range(ends)])  41.5 us
    all_gather x1, blocking collectives, per_device(): group_columns = lax.all_gather(coarsest_columns, 'span', axis=1, tiled=True)  26.1 us
    all_gather x1, blocking collectives, per_device(): lax.all_gather(coarse_rhs, 'span', axis=1, tiled=True)  19.3 us
  transfers between devices with their start and end apart: 53, of which 12 were waited for; matrix products, arithmetic and copies ran while one was open for 2% of the time, Pallas kernels for 0%

commit v1 on v0

--- a/solution.py
+++ b/solution.py
@@ -8,6 +8,13 @@
 KC = 4
 CHEB_CENTRE = 1.0
 CHEB_RADIUS = 0.9
+
+
+def swapped_in(x, name, along):
+    count = lax.axis_size(name)
+    blocks = jnp.stack([x for _ in range(count)])
+    blocks = lax.all_to_all(blocks, name, split_axis=0, concat_axis=0)
+    return jnp.concatenate(blocks, axis=along)
 
 
 def padded(cells, sides, width, closed):
@@ -176,7 +183,7 @@
         lax.all_gather(coarse_rhs, "span", axis=1, tiled=True),
         lax.all_gather(coarsest_values, "span", axis=3, tiled=True),
     )
-    group_columns = lax.all_gather(coarsest_columns, "span", axis=1, tiled=True)
+    group_columns = swapped_in(coarsest_columns, "span", 1)
 
     def group_apply(vector):
         return block_product(group_values, vector[:, group_columns])

time: 707 us -> 692 us (0.979)
  blocking collectives: 45.4 us -> 20.1 us
  starting transfers between devices: 114 us -> 127 us
    all_gather x1 -> x0, blocking collectives: 26.1 us -> none  [per_device(): group_columns = lax.all_gather(coarsest_columns, 'span', axis=1, tiled=True)]
    all_to_all x0 -> x1, starting transfers between devices: none -> 7.63 us  [swapped_in(): blocks = lax.all_to_all(blocks, name, split_axis=0, concat_axis=0)]
  transfers between devices with their start and end apart: 53 -> 54, of which waited for: 12 -> 11; matrix products, arithmetic and copies ran while one was open for 2% -> 16% of each run, Pallas kernels for 0% -> 0%
where the time goes in v1:
time: 692 us; the launch traced here: 682 us
  local copies, waits for them, and re-layouts  211 us (30%)
  matrix products  188 us (27%)
  starting transfers between devices  127 us (18%)
  waiting for transfers between devices  95.9 us (14%)
  other arithmetic  22.8 us (3%)
  blocking collectives  20.1 us (3%)
  between operations  16.8 us (2%)
    dot_general x81, matrix products, one_block(): return jnp.dot(parts, select, preferred_element_type=jnp.float32)  187 us
    gather x3, local copies, waits for them, and re-layouts, group_apply(): return block_product(group_values, vector[:, group_columns])  175 us
    ppermute x26, starting transfers between devices, padded(): lax.ppermute(head, axis, [((i + 1) % count, i) for i in range(ends)])  72.4 us
    all_gather x1, waiting for transfers between devices, per_device(): lax.all_gather(coarsest_values, 'span', axis=3, tiled=True)  50.7 us
    ppermute x26, starting transfers between devices, padded(): lax.ppermute(tail, axis, [(i, (i + 1) % count) for i in range(ends)])  46.4 us
    ppermute x26, waiting for transfers between devices, padded(): lax.ppermute(head, axis, [((i + 1) % count, i) for i in range(ends)])  44.4 us
    all_gather x1, blocking collectives, per_device(): lax.all_gather(coarse_rhs, 'span', axis=1, tiled=True)  20.1 us
    unnamed x87, local copies, waits for them, and re-layouts  17.4 us
  transfers between devices with their start and end apart: 54, of which 11 were waited for; matrix products, arithmetic and copies ran while one was open for 16% of the time, Pallas kernels for 0%

profile of v1, /device:TPU:1, one launch (start us, length us, event | category | flops | bytes accessed | tf_op | source)
XLA Modules:
  0.0 681.7 jit_solution(4092588035808836108)
XLA Ops:
  8.7 50.7 %all-gather.2.cloned.1.call-done = f32[8,4,4,2048]{3,2,1,0:T(4,128)} async-done(((f32[8,4,4,128]{3,2,1,0:T(4,128)}), f32[8,4,4,2048]{3,2,1,0:T(4,128)}) %all-gather.2.cloned.1.call-update) | async-done | bytes 1048592 | tf_op jit(solution)/shard_map/all_gather | solution.py:184
  72.5 7.6 %all-to-all-start = ((s32[16,8,128]{2,1,0:T(8,128)}), s32[16,8,128]{2,1,0:T(8,128)}, u32[]{:S(2)}, u32[]{:S(2)}) async-start(s32[16,8,128]{2,1,0:T(8,128)} %stack.2), calls=%async_computation | async-start | bytes 131072 | tf_op jit(solution)/shard_map/all_to_all | solution.py:16
  82.7 30.0 %while.39 = (s32[]{:T(128)}, f32[8,12,2048]{2,1,0:T(8,128)S(1)}, s32[8,2048]{1,0:T(8,128)}, bf16[12,2304]{1,0:T(8,128)(2,1)S(1)}, s32[]{:T(128)}) while((s32[]{:T(128)}, f32[8,12,2048]{2,1,0:T(8,128)S(1)}, s32[8,2048]{1,0:T(8,128)}, bf16[12,2304]{1,0:T(8,128)(2,1)S(1)}, s32[]{:T(128)}) %tuple.301), condition=%wide.region_2.0_spmd.clone, body=%wide.region_1.0_spmd.clone.sunk | while | flops 117964800 | bytes 229445 | solution.py:89
  114.0 3.6 collective-permute-start.5
  117.5 5.6 collective-permute-start.6
  125.3 6.1 fusion.78
  131.7 23.3 %while.40 = (s32[]{:T(128)}, f32[8,12,2048]{2,1,0:T(8,128)S(1)}, s32[8,2048]{1,0:T(8,128)S(1)}, bf16[12,2304]{1,0:T(8,128)(2,1)S(1)}, s32[]{:T(128)}) while((s32[]{:T(128)}, f32[8,12,2048]{2,1,0:T(8,128)S(1)}, s32[8,2048]{1,0:T(8,128)S(1)}, bf16[12,2304]{1,0:T(8,128)(2,1)S(1)}, s32[]{:T(128)}) %tuple.347), condition=%wide.region_4.5_spmd.clone, body=%wide.region_3.0_spmd.clone.sunk | while | flops 117964800 | bytes 229445 | solution.py:89
  156.2 5.1 collective-permute-start.10
  163.3 3.9 collective-permute-start.9
  170.5 30.5 %while.41 = (s32[]{:T(128)}, f32[8,12,2048]{2,1,0:T(8,128)S(1)}, s32[8,2048]{1,0:T(8,128)S(1)}, bf16[12,2304]{1,0:T(8,128)(2,1)}, s32[]{:T(128)}) while((s32[]{:T(128)}, f32[8,12,2048]{2,1,0:T(8,128)S(1)}, s32[8,2048]{1,0:T(8,128)S(1)}, bf16[12,2304]{1,0:T(8,128)(2,1)}, s32[]{:T(128)}) %tuple.348), condition=%wide.region_7.8_spmd.clone, body=%wide.region_6.7_spmd.clone.sunk | while | flops 117964800 | bytes 211013 | solution.py:89
  170.5 3.9 fusion.397
  174.4 3.8 fusion.397
  178.2 3.8 fusion.397
  182.0 3.8 fusion.397
  185.8 3.8 fusion.397
  189.6 3.8 fusion.397
  193.4 3.8 fusion.397
  197.2 3.8 fusion.397
  203.5 3.6 collective-permute-start.13
  207.1 6.3 collective-permute-start.14
  222.8 3.6 collective-permute-start.17
  231.8 4.0 collective-permute-done.19
  238.8 3.6 collective-permute-start.21
  247.1 5.1 collective-permute-done.23
  255.1 20.1 %all_gather.7 = f32[4,2048]{1,0:T(4,128)S(1)} all-gather(f32[4,128]{1,0:T(4,128)S(1)} %slice_add_fusion.58), channel_id=1, replica_groups=mesh['stream'=8,'span'=16] {'span'}, dimensions={1}, use_global_device_ids=true | all-gather | bytes 34816 | tf_op jit(solution)/shard_map/all_gather | solution.py:183
  276.2 54.8 %gather_fusion = f32[16384,4]{1,0:T(8,128)} fusion(f32[4,2048]{0,1:T(8,128)S(1)} %copy.181, s32[16384]{0:T(1024)S(1)} %broadcast_clamp_fusion), kind=kCustom, calls=%fused_computation | custom fusion | bytes 589824 | tf_op jit(solution)/shard_map/gather | solution.py:189
  331.0 5.3 copy.404
  339.0 60.0 %gather_fusion.1 = f32[16384,4]{1,0:T(8,128)} fusion(f32[4,2048]{0,1:T(8,128)S(1)} %copy.182, s32[16384]{0:T(1024)} %copy-done.5), kind=kCustom, calls=%fused_computation.1 | custom fusion | bytes 589824 | tf_op jit(solution)/shard_map/gather | solution.py:189
  399.1 5.2 copy.405
  406.5 60.0 %gather_fusion.2 = f32[16384,4]{1,0:T(8,128)} fusion(f32[4,2048]{0,1:T(8,128)S(1)} %copy.183, s32[16384]{0:T(1024)} %copy-done.5), kind=kCustom, calls=%fused_computation.2 | custom fusion | bytes 589824 | tf_op jit(solution)/shard_map/gather | solution.py:189
  466.5 5.3 copy.406
  473.5 3.6 collective-permute-start.25
  477.1 5.2 collective-permute-start.26
  484.2 4.4 collective-permute-done.27
  491.7 3.6 collective-permute-start.29
  499.8 4.4 collective-permute-done.31
  507.3 3.6 collective-permute-start.33
  515.6 4.2 collective-permute-done.35
  524.1 3.6 collective-permute-start.37
  532.1 4.4 collective-permute-done.39
  536.9 23.3 %while.48 = (s32[]{:T(128)}, f32[8,12,2048]{2,1,0:T(8,128)S(1)}, s32[8,2048]{1,0:T(8,128)S(1)}, bf16[12,2304]{1,0:T(8,128)(2,1)S(1)}, s32[]{:T(128)}) while((s32[]{:T(128)}, f32[8,12,2048]{2,1,0:T(8,128)S(1)}, s32[8,2048]{1,0:T(8,128)S(1)}, bf16[12,2304]{1,0:T(8,128)(2,1)S(1)}, s32[]{:T(128)}) %tuple.349), condition=%wide.region_24.25_spmd.clone, body=%wide.region_23.24_spmd.clone.sunk | while | flops 117964800 | bytes 229445 | solution.py:89
  561.3 3.6 collective-permute-start.41
  569.6 4.2 collective-permute-done.43
  574.1 23.3 %while.49 = (s32[]{:T(128)}, f32[8,12,2048]{2,1,0:T(8,128)S(1)}, s32[8,2048]{1,0:T(8,128)S(1)}, bf16[12,2304]{1,0:T(8,128)(2,1)S(1)}, s32[]{:T(128)}) while((s32[]{:T(128)}, f32[8,12,2048]{2,1,0:T(8,128)S(1)}, s32[8,2048]{1,0:T(8,128)S(1)}, bf16[12,2304]{1,0:T(8,128)(2,1)S(1)}, s32[]{:T(128)}) %tuple.350), condition=%wide.region_26.27_spmd.clone, body=%wide.region_25.26_spmd.clone.sunk | while | flops 117964800 | bytes 229445 | solution.py:89
  606.6 4.9 collective-permute-done.47
  611.8 23.3 %while.50 = (s32[]{:T(128)}, f32[8,12,2048]{2,1,0:T(8,128)S(1)}, s32[8,2048]{1,0:T(8,128)S(1)}, bf16[12,2304]{1,0:T(8,128)(2,1)S(1)}, s32[]{:T(128)}) while((s32[]{:T(128)}, f32[8,12,2048]{2,1,0:T(8,128)S(1)}, s32[8,2048]{1,0:T(8,128)S(1)}, bf16[12,2304]{1,0:T(8,128)(2,1)S(1)}, s32[]{:T(128)}) %tuple.351), condition=%wide.region_28.29_spmd.clone, body=%wide.region_27.28_spmd.clone.sunk | while | flops 117964800 | bytes 229445 | solution.py:89
  644.6 5.1 collective-permute-done.51
  650.0 23.3 %while.51 = (s32[]{:T(128)}, f32[8,12,2048]{2,1,0:T(8,128)S(1)}, s32[8,2048]{1,0:T(8,128)S(1)}, bf16[12,2304]{1,0:T(8,128)(2,1)S(1)}, s32[]{:T(128)}) while((s32[]{:T(128)}, f32[8,12,2048]{2,1,0:T(8,128)S(1)}, s32[8,2048]{1,0:T(8,128)S(1)}, bf16[12,2304]{1,0:T(8,128)(2,1)S(1)}, s32[]{:T(128)}) %tuple.352), condition=%wide.region_30.31_spmd.clone, body=%wide.region_29.30_spmd.clone.sunk | while | flops 117964800 | bytes 229445 | solution.py:89
  (560 shorter events, 272.7 us)
Async XLA Ops:
  7.2 52.2 %all-gather.2.cloned.1.call-start = ((), (), s32[]{:S(2)}) async-start(), calls=%async_computation.1 | async-start | bytes 1114112 | tf_op jit(solution)/shard_map/all_gather | solution.py:184
  62.6 19.7 %collective-permute-start = (f32[4,64]{1,0:T(4,128)S(1)}, f32[4,64]{1,0:T(4,128)S(1)}, u32[]{:S(2)}, u32[]{:S(2)}) collective-permute-start(f32[4,64]{1,0:T(4,128)S(1)} %bitcast.686), channel_id=1, source_target_pairs={{0,16},{16,32},{32,48},{48,64},{64,80},{80,96},{96,112},{112,0},{1... | collective-permute-start | bytes 3080 | tf_op jit(solution)/shard_map/ppermute | solution.py:28
  63.1 19.3 %collective-permute-start.1 = (f32[4,64]{1,0:T(4,128)S(1)}, f32[4,64]{1,0:T(4,128)S(1)}, u32[]{:S(2)}, u32[]{:S(2)}) collective-permute-start(f32[4,64]{1,0:T(4,128)S(1)} %bitcast.683), channel_id=1, source_target_pairs={{16,0},{32,16},{48,32},{64,48},{80,64},{96,80},{112,96},{0,112},{1... | collective-permute-start | bytes 3080 | tf_op jit(solution)/shard_map/ppermute | solution.py:30
  66.3 16.1 %collective-permute-start.2 = (f32[4,64]{1,0:T(4,128)S(1)}, f32[4,64]{1,0:T(4,128)S(1)}, u32[]{:S(2)}, u32[]{:S(2)}) collective-permute-start(f32[4,64]{1,0:T(4,128)S(1)} %bitcast.681), channel_id=1, source_target_pairs={{0,1},{1,2},{2,3},{3,4},{4,5},{5,6},{6,7},{7,8},{8,9},{9,10},{10,1... | collective-permute-start | bytes 3080 | tf_op jit(solution)/shard_map/ppermute | solution.py:28
  69.2 13.2 %collective-permute-start.3 = (f32[4,64]{1,0:T(4,128)S(1)}, f32[4,64]{1,0:T(4,128)S(1)}, u32[]{:S(2)}, u32[]{:S(2)}) collective-permute-start(f32[4,64]{1,0:T(4,128)S(1)} %bitcast.679), channel_id=1, source_target_pairs={{1,0},{2,1},{3,2},{4,3},{5,4},{6,5},{7,6},{8,7},{9,8},{10,9},{11,1... | collective-permute-start | bytes 3080 | tf_op jit(solution)/shard_map/ppermute | solution.py:30
  72.5 158.4 %all-to-all-start = ((s32[16,8,128]{2,1,0:T(8,128)}), s32[16,8,128]{2,1,0:T(8,128)}, u32[]{:S(2)}, u32[]{:S(2)}) async-start(s32[16,8,128]{2,1,0:T(8,128)} %stack.2), calls=%async_computation | async-start | bytes 131072 | tf_op jit(solution)/shard_map/all_to_all | solution.py:16
  113.9 17.5 %collective-permute-start.4 = (f32[4,64]{1,0:T(4,128)S(1)}, f32[4,64]{1,0:T(4,128)S(1)}, u32[]{:S(2)}, u32[]{:S(2)}) collective-permute-start(f32[4,64]{1,0:T(4,128)S(1)} %bitcast.718), channel_id=1, source_target_pairs={{0,16},{16,32},{32,48},{48,64},{64,80},{80,96},{96,112},{112,0},{1... | collective-permute-start | bytes 3080 | tf_op jit(solution)/shard_map/ppermute | solution.py:28
  114.0 17.4 %collective-permute-start.5 = (f32[4,64]{1,0:T(4,128)S(1)}, f32[4,64]{1,0:T(4,128)S(1)}, u32[]{:S(2)}, u32[]{:S(2)}) collective-permute-start(f32[4,64]{1,0:T(4,128)S(1)} %bitcast.709), channel_id=1, source_target_pairs={{16,0},{32,16},{48,32},{64,48},{80,64},{96,80},{112,96},{0,112},{1... | collective-permute-start | bytes 3080 | tf_op jit(solution)/shard_map/ppermute | solution.py:30
  117.5 13.9 %collective-permute-start.6 = (f32[4,64]{1,0:T(4,128)S(1)}, f32[4,64]{1,0:T(4,128)S(1)}, u32[]{:S(2)}, u32[]{:S(2)}) collective-permute-start(f32[4,64]{1,0:T(4,128)S(1)} %bitcast.699), channel_id=1, source_target_pairs={{0,1},{1,2},{2,3},{3,4},{4,5},{5,6},{6,7},{7,8},{8,9},{9,10},{10,1... | collective-permute-start | bytes 3080 | tf_op jit(solution)/shard_map/ppermute | solution.py:28
  123.1 8.3 %collective-permute-start.7 = (f32[4,64]{1,0:T(4,128)S(1)}, f32[4,64]{1,0:T(4,128)S(1)}, u32[]{:S(2)}, u32[]{:S(2)}) collective-permute-start(f32[4,64]{1,0:T(4,128)S(1)} %bitcast.689), channel_id=1, source_target_pairs={{1,0},{2,1},{3,2},{4,3},{5,4},{6,5},{7,6},{8,7},{9,8},{10,9},{11,1... | collective-permute-start | bytes 3080 | tf_op jit(solution)/shard_map/ppermute | solution.py:30
  156.2 13.3 %collective-permute-start.10 = (f32[4,64]{1,0:T(4,128)S(1)}, f32[4,64]{1,0:T(4,128)S(1)}, u32[]{:S(2)}, u32[]{:S(2)}) collective-permute-start(f32[4,64]{1,0:T(4,128)S(1)} %bitcast.692), channel_id=1, source_target_pairs={{0,1},{1,2},{2,3},{3,4},{4,5},{5,6},{6,7},{7,8},{8,9},{9,10},{10,1... | collective-permute-start | bytes 3080 | tf_op jit(solution)/shard_map/ppermute | solution.py:28
  161.3 8.2 %collective-permute-start.11 = (f32[4,64]{1,0:T(4,128)S(1)}, f32[4,64]{1,0:T(4,128)S(1)}, u32[]{:S(2)}, u32[]{:S(2)}) collective-permute-start(f32[4,64]{1,0:T(4,128)S(1)} %bitcast.688), channel_id=1, source_target_pairs={{1,0},{2,1},{3,2},{4,3},{5,4},{6,5},{7,6},{8,7},{9,8},{10,9},{11,1... | collective-permute-start | bytes 3080 | tf_op jit(solution)/shard_map/ppermute | solution.py:30
  163.2 6.2 collective-permute-start.8
  163.3 6.2 collective-permute-start.9
  203.4 12.8 %collective-permute-start.12 = (f32[4,64]{1,0:T(4,128)S(1)}, f32[4,64]{1,0:T(4,128)S(1)}, u32[]{:S(2)}, u32[]{:S(2)}) collective-permute-start(f32[4,64]{1,0:T(4,128)S(1)} %bitcast.680), channel_id=1, source_target_pairs={{0,16},{16,32},{32,48},{48,64},{64,80},{80,96},{96,112},{112,0},{1... | collective-permute-start | bytes 3080 | tf_op jit(solution)/shard_map/ppermute | solution.py:28
  203.5 12.7 %collective-permute-start.13 = (f32[4,64]{1,0:T(4,128)S(1)}, f32[4,64]{1,0:T(4,128)S(1)}, u32[]{:S(2)}, u32[]{:S(2)}) collective-permute-start(f32[4,64]{1,0:T(4,128)S(1)} %bitcast.678), channel_id=1, source_target_pairs={{16,0},{32,16},{48,32},{64,48},{80,64},{96,80},{112,96},{0,112},{1... | collective-permute-start | bytes 3080 | tf_op jit(solution)/shard_map/ppermute | solution.py:30
  207.1 9.1 %collective-permute-start.14 = (f32[4,64]{1,0:T(4,128)S(1)}, f32[4,64]{1,0:T(4,128)S(1)}, u32[]{:S(2)}, u32[]{:S(2)}) collective-permute-start(f32[4,64]{1,0:T(4,128)S(1)} %bitcast.677), channel_id=1, source_target_pairs={{0,1},{1,2},{2,3},{3,4},{4,5},{5,6},{6,7},{7,8},{8,9},{9,10},{10,1... | collective-permute-start | bytes 3080 | tf_op jit(solution)/shard_map/ppermute | solution.py:28
  213.3 6.4 collective-permute-start.15
  222.8 9.0 %collective-permute-start.16 = (f32[4,64]{1,0:T(4,128)S(1)}, f32[4,64]{1,0:T(4,128)S(1)}, u32[]{:S(2)}, u32[]{:S(2)}) collective-permute-start(f32[4,64]{1,0:T(4,128)S(1)} %bitcast.700), channel_id=1, source_target_pairs={{0,16},{16,32},{32,48},{48,64},{64,80},{80,96},{96,112},{112,0},{1... | collective-permute-start | bytes 3080 | tf_op jit(solution)/shard_map/ppermute | solution.py:28
  222.8 8.9 %collective-permute-start.17 = (f32[4,64]{1,0:T(4,128)S(1)}, f32[4,64]{1,0:T(4,128)S(1)}, u32[]{:S(2)}, u32[]{:S(2)}) collective-permute-start(f32[4,64]{1,0:T(4,128)S(1)} %bitcast.690), channel_id=1, source_target_pairs={{16,0},{32,16},{48,32},{64,48},{80,64},{96,80},{112,96},{0,112},{1... | collective-permute-start | bytes 3080 | tf_op jit(solution)/shard_map/ppermute | solution.py:30
  226.4 5.3 collective-permute-start.18
  228.9 6.8 %collective-permute-start.19 = (f32[4,64]{1,0:T(4,128)S(1)}, f32[4,64]{1,0:T(4,128)S(1)}, u32[]{:S(2)}, u32[]{:S(2)}) collective-permute-start(f32[4,64]{1,0:T(4,128)S(1)} %bitcast.684), channel_id=1, source_target_pairs={{1,0},{2,1},{3,2},{4,3},{5,4},{6,5},{7,6},{8,7},{9,8},{10,9},{11,1... | collective-permute-start | bytes 3080 | tf_op jit(solution)/shard_map/ppermute | solution.py:30
  238.8 8.3 %collective-permute-start.20 = (f32[4,64]{1,0:T(4,128)S(1)}, f32[4,64]{1,0:T(4,128)S(1)}, u32[]{:S(2)}, u32[]{:S(2)}) collective-permute-start(f32[4,64]{1,0:T(4,128)S(1)} %bitcast.720), channel_id=1, source_target_pairs={{0,16},{16,32},{32,48},{48,64},{64,80},{80,96},{96,112},{112,0},{1... | collective-permute-start | bytes 3080 | tf_op jit(solution)/shard_map/ppermute | solution.py:28
  238.8 8.2 %collective-permute-start.21 = (f32[4,64]{1,0:T(4,128)S(1)}, f32[4,64]{1,0:T(4,128)S(1)}, u32[]{:S(2)}, u32[]{:S(2)}) collective-permute-start(f32[4,64]{1,0:T(4,128)S(1)} %bitcast.711), channel_id=1, source_target_pairs={{16,0},{32,16},{48,32},{64,48},{80,64},{96,80},{112,96},{0,112},{1... | collective-permute-start | bytes 3080 | tf_op jit(solution)/shard_map/ppermute | solution.py:30
  244.9 7.3 %collective-permute-start.23 = (f32[4,64]{1,0:T(4,128)S(1)}, f32[4,64]{1,0:T(4,128)S(1)}, u32[]{:S(2)}, u32[]{:S(2)}) collective-permute-start(f32[4,64]{1,0:T(4,128)S(1)} %bitcast.691), channel_id=1, source_target_pairs={{1,0},{2,1},{3,2},{4,3},{5,4},{6,5},{7,6},{8,7},{9,8},{10,9},{11,1... | collective-permute-start | bytes 3080 | tf_op jit(solution)/shard_map/ppermute | solution.py:30
  473.4 10.7 %collective-permute-start.24 = (f32[4,64]{1,0:T(4,128)S(1)}, f32[4,64]{1,0:T(4,128)S(1)}, u32[]{:S(2)}, u32[]{:S(2)}) collective-permute-start(f32[4,64]{1,0:T(4,128)S(1)} %bitcast.721), channel_id=1, source_target_pairs={{0,16},{16,32},{32,48},{48,64},{64,80},{80,96},{96,112},{112,0},{1... | collective-permute-start | bytes 3080 | tf_op jit(solution)/shard_map/ppermute | solution.py:28
  473.5 10.7 %collective-permute-start.25 = (f32[4,64]{1,0:T(4,128)S(1)}, f32[4,64]{1,0:T(4,128)S(1)}, u32[]{:S(2)}, u32[]{:S(2)}) collective-permute-start(f32[4,64]{1,0:T(4,128)S(1)} %bitcast.712), channel_id=1, source_target_pairs={{16,0},{32,16},{48,32},{64,48},{80,64},{96,80},{112,96},{0,112},{1... | collective-permute-start | bytes 3080 | tf_op jit(solution)/shard_map/ppermute | solution.py:30
  477.1 7.1 %collective-permute-start.26 = (f32[4,64]{1,0:T(4,128)S(1)}, f32[4,64]{1,0:T(4,128)S(1)}, u32[]{:S(2)}, u32[]{:S(2)}) collective-permute-start(f32[4,64]{1,0:T(4,128)S(1)} %bitcast.703), channel_id=1, source_target_pairs={{0,1},{1,2},{2,3},{3,4},{4,5},{5,6},{6,7},{7,8},{8,9},{9,10},{10,1... | collective-permute-start | bytes 3080 | tf_op jit(solution)/shard_map/ppermute | solution.py:28
  482.2 6.4 collective-permute-start.27
  491.7 8.1 %collective-permute-start.28 = (f32[4,64]{1,0:T(4,128)S(1)}, f32[4,64]{1,0:T(4,128)S(1)}, u32[]{:S(2)}, u32[]{:S(2)}) collective-permute-start(f32[4,64]{1,0:T(4,128)S(1)} %bitcast.722), channel_id=1, source_target_pairs={{0,16},{16,32},{32,48},{48,64},{64,80},{80,96},{96,112},{112,0},{1... | collective-permute-start | bytes 3080 | tf_op jit(solution)/shard_map/ppermute | solution.py:28
  491.7 8.0 %collective-permute-start.29 = (f32[4,64]{1,0:T(4,128)S(1)}, f32[4,64]{1,0:T(4,128)S(1)}, u32[]{:S(2)}, u32[]{:S(2)}) collective-permute-start(f32[4,64]{1,0:T(4,128)S(1)} %bitcast.713), channel_id=1, source_target_pairs={{16,0},{32,16},{48,32},{64,48},{80,64},{96,80},{112,96},{0,112},{1... | collective-permute-start | bytes 3080 | tf_op jit(solution)/shard_map/ppermute | solution.py:30
  497.8 6.4 collective-permute-start.31
  507.2 8.3 %collective-permute-start.32 = (f32[4,64]{1,0:T(4,128)S(1)}, f32[4,64]{1,0:T(4,128)S(1)}, u32[]{:S(2)}, u32[]{:S(2)}) collective-permute-start(f32[4,64]{1,0:T(4,128)S(1)} %bitcast.723), channel_id=1, source_target_pairs={{0,16},{16,32},{32,48},{48,64},{64,80},{80,96},{96,112},{112,0},{1... | collective-permute-start | bytes 3080 | tf_op jit(solution)/shard_map/ppermute | solution.py:28
  507.3 8.2 %collective-permute-start.33 = (f32[4,64]{1,0:T(4,128)S(1)}, f32[4,64]{1,0:T(4,128)S(1)}, u32[]{:S(2)}, u32[]{:S(2)}) collective-permute-start(f32[4,64]{1,0:T(4,128)S(1)} %bitcast.714), channel_id=1, source_target_pairs={{16,0},{32,16},{48,32},{64,48},{80,64},{96,80},{112,96},{0,112},{1... | collective-permute-start | bytes 3080 | tf_op jit(solution)/shard_map/ppermute | solution.py:30
  513.4 6.4 collective-permute-start.35
  524.0 8.1 %collective-permute-start.36 = (f32[4,64]{1,0:T(4,128)S(1)}, f32[4,64]{1,0:T(4,128)S(1)}, u32[]{:S(2)}, u32[]{:S(2)}) collective-permute-start(f32[4,64]{1,0:T(4,128)S(1)} %bitcast.724), channel_id=1, source_target_pairs={{0,16},{16,32},{32,48},{48,64},{64,80},{80,96},{96,112},{112,0},{1... | collective-permute-start | bytes 3080 | tf_op jit(solution)/shard_map/ppermute | solution.py:28
  524.1 8.0 %collective-permute-start.37 = (f32[4,64]{1,0:T(4,128)S(1)}, f32[4,64]{1,0:T(4,128)S(1)}, u32[]{:S(2)}, u32[]{:S(2)}) collective-permute-start(f32[4,64]{1,0:T(4,128)S(1)} %bitcast.715), channel_id=1, source_target_pairs={{16,0},{32,16},{48,32},{64,48},{80,64},{96,80},{112,96},{0,112},{1... | collective-permute-start | bytes 3080 | tf_op jit(solution)/shard_map/ppermute | solution.py:30
  530.1 6.4 collective-permute-start.39
  561.2 8.3 %collective-permute-start.40 = (f32[4,64]{1,0:T(4,128)S(1)}, f32[4,64]{1,0:T(4,128)S(1)}, u32[]{:S(2)}, u32[]{:S(2)}) collective-permute-start(f32[4,64]{1,0:T(4,128)S(1)} %bitcast.725), channel_id=1, source_target_pairs={{0,16},{16,32},{32,48},{48,64},{64,80},{80,96},{96,112},{112,0},{1... | collective-permute-start | bytes 3080 | tf_op jit(solution)/shard_map/ppermute | solution.py:28
  561.3 8.3 %collective-permute-start.41 = (f32[4,64]{1,0:T(4,128)S(1)}, f32[4,64]{1,0:T(4,128)S(1)}, u32[]{:S(2)}, u32[]{:S(2)}) collective-permute-start(f32[4,64]{1,0:T(4,128)S(1)} %bitcast.716), channel_id=1, source_target_pairs={{16,0},{32,16},{48,32},{64,48},{80,64},{96,80},{112,96},{0,112},{1... | collective-permute-start | bytes 3080 | tf_op jit(solution)/shard_map/ppermute | solution.py:30
  567.4 6.4 collective-permute-start.43
  598.5 8.1 %collective-permute-start.44 = (f32[4,64]{1,0:T(4,128)S(1)}, f32[4,64]{1,0:T(4,128)S(1)}, u32[]{:S(2)}, u32[]{:S(2)}) collective-permute-start(f32[4,64]{1,0:T(4,128)S(1)} %bitcast.726), channel_id=1, source_target_pairs={{0,16},{16,32},{32,48},{48,64},{64,80},{80,96},{96,112},{112,0},{1... | collective-permute-start | bytes 3080 | tf_op jit(solution)/shard_map/ppermute | solution.py:28
  598.6 8.0 %collective-permute-start.45 = (f32[4,64]{1,0:T(4,128)S(1)}, f32[4,64]{1,0:T(4,128)S(1)}, u32[]{:S(2)}, u32[]{:S(2)}) collective-permute-start(f32[4,64]{1,0:T(4,128)S(1)} %bitcast.717), channel_id=1, source_target_pairs={{16,0},{32,16},{48,32},{64,48},{80,64},{96,80},{112,96},{0,112},{1... | collective-permute-start | bytes 3080 | tf_op jit(solution)/shard_map/ppermute | solution.py:30
  604.7 6.8 %collective-permute-start.47 = (f32[4,64]{1,0:T(4,128)S(1)}, f32[4,64]{1,0:T(4,128)S(1)}, u32[]{:S(2)}, u32[]{:S(2)}) collective-permute-start(f32[4,64]{1,0:T(4,128)S(1)} %bitcast.698), channel_id=1, source_target_pairs={{1,0},{2,1},{3,2},{4,3},{5,4},{6,5},{7,6},{8,7},{9,8},{10,9},{11,1... | collective-permute-start | bytes 3080 | tf_op jit(solution)/shard_map/ppermute | solution.py:30
  636.2 8.4 %collective-permute-start.48 = (f32[4,64]{1,0:T(4,128)S(1)}, f32[4,64]{1,0:T(4,128)S(1)}, u32[]{:S(2)}, u32[]{:S(2)}) collective-permute-start(f32[4,64]{1,0:T(4,128)S(1)} %bitcast.727), channel_id=1, source_target_pairs={{0,16},{16,32},{32,48},{48,64},{64,80},{80,96},{96,112},{112,0},{1... | collective-permute-start | bytes 3080 | tf_op jit(solution)/shard_map/ppermute | solution.py:28
  636.3 8.3 %collective-permute-start.49 = (f32[4,64]{1,0:T(4,128)S(1)}, f32[4,64]{1,0:T(4,128)S(1)}, u32[]{:S(2)}, u32[]{:S(2)}) collective-permute-start(f32[4,64]{1,0:T(4,128)S(1)} %bitcast.719), channel_id=1, source_target_pairs={{16,0},{32,16},{48,32},{64,48},{80,64},{96,80},{112,96},{0,112},{1... | collective-permute-start | bytes 3080 | tf_op jit(solution)/shard_map/ppermute | solution.py:30
  639.9 4.8 collective-permute-start.50
  642.4 7.3 %collective-permute-start.51 = (f32[4,64]{1,0:T(4,128)S(1)}, f32[4,64]{1,0:T(4,128)S(1)}, u32[]{:S(2)}, u32[]{:S(2)}) collective-permute-start(f32[4,64]{1,0:T(4,128)S(1)} %bitcast.701), channel_id=1, source_target_pairs={{1,0},{2,1},{3,2},{4,3},{5,4},{6,5},{7,6},{8,7},{9,8},{10,9},{11,1... | collective-permute-start | bytes 3080 | tf_op jit(solution)/shard_map/ppermute | solution.py:30
  (44 other events, 772.8 us)
Sparse Core Ops, SparseCore 0:
  10.3 49.1 all-gather.1
